TPU v7x, 128 devices: a whole 4x4x4 slice. The times are simulated.
128 devices in a mesh: req: 16 (over x, y), row: 8 (over z, core).
Axes of the slice: x: 4, y: 4, z: 4, core: 2. Of those that a mesh axis runs over, the one named last changes fastest.
Arguments:
- patches: bfloat16 [8, 2048, 1280], P('row', 'req'), may hold values from -6 to 6
- picture_ids: int32 [8, 2048], P('row'), may hold values from -1 to 15, as said below
- ln_attn: float32 [1280], replicated, may hold values from 0.1 to 1.9
- w_qkv: bfloat16 [3, 1280, 1280], P(None, None, 'req'), may hold values from -6 to 6
- w_out: bfloat16 [1280, 1280], P('req'), may hold values from -1.25 to 1.25
- ln_mlp: float32 [1280], replicated, may hold values from 0.1 to 1.9
- w_up: bfloat16 [1280, 5120], P(None, 'req'), may hold values from -0.15625 to 0.15625
- w_down: bfloat16 [5120, 1280], P('req'), may hold values from -0.3125 to 0.3125
- w_merge: bfloat16 [5120, 1280], replicated, may hold values from -0.078125 to 0.078125
- text_embed: bfloat16 [16384, 1280], P(('req', 'row')), may hold values from -6 to 6
- slot_dest: int32 [8, 512], P('row', 'req'), may hold values from -1 to 16383, as said below
Outputs:
- prompt_embed: bfloat16 [16384, 1280], P(('req', 'row'))
Inputs may be any that keep to these rules, and one draw needn't show every extreme that they name: `picture_ids`: each group holds whole pictures one after another from its first row, each picture's length a multiple of 4 and laid out so that every aligned run of four rows is one 2x2 window; rows after the last picture are padding. `slot_dest`: A merged row has a prompt row exactly when its patch rows belong to a picture; no prompt row is named twice; a merged row of group g (rows of the row index g) names a prompt row of a device with the same row index; at most 2 merged rows of one device name prompt rows of one device, and in every draw some device sends that many to one device.
All inputs are finite; a program needn't handle non-finite values.
Results may differ from a plain program's by a relative error of at most 0.023.
Values may be sent and summed in bfloat16 or wider, within the bound.
No kernel may reach another device: no remote copies, remote signals or barrier semaphores. Data moves between devices by JAX's collectives and lax.ppermute only.
A program may use at most 128 MiB of HBM per device.

v0:
```python
import math
import jax
import jax.numpy as jnp
from jax import lax
from jax.sharding import PartitionSpec as P

HEAD = 80


def layer_norm(rows, gain):
    rows32 = rows.astype(jnp.float32)
    center = rows32 - jnp.mean(rows32, axis=-1, keepdims=True)
    spread = jnp.mean(center * center, axis=-1, keepdims=True)
    return center * lax.rsqrt(spread + 1e-06) * gain


def local(
    patches,
    picture_ids,
    ln_attn,
    w_qkv,
    w_out,
    ln_mlp,
    w_up,
    w_down,
    w_merge,
    text_embed,
    slot_dest,
):
    rows = patches[0]
    local_rows = rows.shape[0]
    width = rows.shape[1]
    ids = picture_ids[0]
    group_rows = ids.shape[0]
    head_cols = w_out.shape[0]
    req_count = lax.axis_size("req")
    row_count = lax.axis_size("row")
    normed = layer_norm(rows, ln_attn).astype(jnp.bfloat16)
    qkv = jnp.einsum(
        "rd,tdc->trc",
        lax.all_gather(normed, "req", axis=0, tiled=True),
        w_qkv,
        preferred_element_type=jnp.float32,
    ).astype(jnp.bfloat16)
    keys = qkv[1]
    values = qkv[2]
    block = min(512, group_rows)
    blocks = group_rows // block
    scale = 1.0 / math.sqrt(HEAD)

    def attend(item):
        query_block, id_block = item
        same = id_block[:, None] == ids[None, :]
        scores = (
            jnp.einsum("qc,kc->qk", query_block, keys, preferred_element_type=jnp.float32) * scale
        )
        scores = jnp.where(same, scores, -1e30)
        top = jnp.max(scores, axis=1, keepdims=True)
        expo = jnp.exp(scores - top)
        probs = (expo / jnp.sum(expo, axis=1, keepdims=True)).astype(jnp.bfloat16)
        results = [jnp.dot(probs, values, preferred_element_type=jnp.float32).astype(jnp.bfloat16)]
        return jnp.concatenate(results, axis=1)

    attended = lax.map(
        attend, (qkv[0].reshape(blocks, block, head_cols), ids.reshape(blocks, block))
    )
    attended = attended.reshape(group_rows, head_cols)
    piece = lax.slice_in_dim(attended, 0, local_rows * lax.axis_size("req"), axis=0)
    attn = lax.psum_scatter(
        jnp.dot(piece, w_out, preferred_element_type=jnp.float32).astype(jnp.bfloat16),
        "req",
        scatter_dimension=0,
        tiled=True,
    ).astype(jnp.float32)
    resid = (rows.astype(jnp.float32) + attn).astype(jnp.bfloat16)
    normed_two = layer_norm(resid, ln_mlp).astype(jnp.bfloat16)
    hidden = jax.nn.gelu(
        jnp.dot(
            lax.all_gather(normed_two, "req", axis=0, tiled=True),
            w_up,
            preferred_element_type=jnp.float32,
        ),
        approximate=False,
    ).astype(jnp.bfloat16)
    piece = lax.slice_in_dim(hidden, 0, local_rows * lax.axis_size("req"), axis=0)
    mlp = lax.psum_scatter(
        jnp.dot(piece, w_down, preferred_element_type=jnp.float32).astype(jnp.bfloat16),
        "req",
        scatter_dimension=0,
        tiled=True,
    ).astype(jnp.float32)
    vision = (resid.astype(jnp.float32) + mlp).astype(jnp.bfloat16)
    merged = vision.reshape(local_rows // 4, 4 * width)
    merged_count = merged.shape[0]
    dest = slot_dest[0]
    prompt_rows = text_embed.shape[0]
    slot_cap = max(2, merged_count // req_count)
    owner = jnp.where(dest >= 0, dest // prompt_rows // row_count, -1)
    order = jnp.arange(merged_count)
    same_owner = (owner[:, None] == owner[None, :]) & (order[None, :] < order[:, None])
    ranks = jnp.sum(same_owner.astype(jnp.int32), axis=1)
    target = jnp.where(owner >= 0, owner * slot_cap + ranks, -1)
    select = target[None, :] == jnp.arange(req_count * slot_cap)[:, None]
    places = jnp.sum(jnp.where(select, (dest % prompt_rows + 1)[None, :], 0), axis=1) - 1
    chooser = select.astype(jnp.bfloat16)
    outgoing = jnp.dot(chooser, merged, preferred_element_type=jnp.float32).astype(jnp.bfloat16)
    arrived, landing = (
        lax.all_to_all(
            outgoing.reshape(req_count, slot_cap, -1),
            "req",
            split_axis=0,
            concat_axis=0,
            tiled=True,
        ),
        lax.all_to_all(
            places.reshape(req_count, slot_cap), "req", split_axis=0, concat_axis=0, tiled=True
        ),
    )
    arrived = arrived.reshape(req_count * slot_cap, -1)
    landing = landing.reshape(-1)
    incoming = jnp.dot(arrived, w_merge, preferred_element_type=jnp.float32).astype(jnp.bfloat16)
    placer = landing[None, :] == jnp.arange(prompt_rows)[:, None]
    placed = jnp.dot(
        placer.astype(jnp.bfloat16), incoming, preferred_element_type=jnp.float32
    ).astype(jnp.bfloat16)
    filled = jnp.any(placer, axis=1)
    return jnp.where(filled[:, None], placed, text_embed)


def solution(mesh):
    return jax.shard_map(
        local,
        mesh=mesh,
        in_specs=(
            P("row", "req", None),
            P("row", None),
            P(),
            P(None, None, "req"),
            P("req", None),
            P(),
            P(None, "req"),
            P("req", None),
            P(),
            P(("req", "row"), None),
            P("row", "req"),
        ),
        out_specs=P(("req", "row"), None),
        check_vma=False,
    )
```

profile of v0, /device:TPU:0, one launch (start us, length us, event | category | flops | bytes accessed | tf_op | source)
XLA Modules:
  0.0 349.8 jit_solution(17088282344082328541)
XLA Ops:
  6.5 0.0 copy-start
  6.5 1.2 convert_reduce_fusion.1
  7.7 1.2 fusion.59
  8.9 1.9 fusion.61
  10.9 0.0 all-gather.3.cloned.1.call-update
  10.9 0.0 reduce-scatter.3.cloned.1.call-start
  11.0 0.6 broadcast.226
  11.5 1.4 reduce.7
  12.9 56.8 %all-gather.3.cloned.1.call-done = bf16[2048,1280]{1,0:T(8,128)(2,1)} async-done(((bf16[128,1280]{1,0:T(8,128)(2,1)}), bf16[2048,1280]{1,0:T(8,128)(2,1)}) %all-gather.3.cloned.1.call-update) | async-done | bytes 5242896 | tf_op jit(solution)/shard_map/all_gather | solution.py:41
  69.8 4.2 %fusion.105 = f32[2048,240]{0,1:S(1)} fusion(bf16[2048,1280]{1,0:T(8,128)(2,1)} %all-gather.3.cloned.1.call-done, bf16[1280,240]{0,1:T(8,128)(2,1)} %bitcast.94), kind=kOutput, calls=%fused_computation.160 | convolution fusion | flops 1258291200 | bytes 7823360
  73.9 0.1 convert_bitcast_fusion
  74.1 0.0 copy-start.4
  74.1 0.1 slice_bitcast_fusion
  74.2 0.3 copy.29
  74.4 0.3 copy.26
  74.7 0.3 copy.27
  75.0 0.0 copy-done.4
  75.0 0.0 copy-start.3
  75.0 11.0 %while.10 = (s32[]{:T(128)}, bf16[4,512,80]{1,2,0:T(8,128)(2,1)S(1)}, s32[4,512]{1,0:T(4,128)S(1)}, s32[1,2048]{1,0:T(1,128)S(1)}, bf16[4,512,80]{2,1,0:T(8,128)...) while((s32[]{:T(128)}, bf16[4,512,80]{1,2,0:T(8,128)(2,1)S(1)}, ...), condition=%wide.region_8.9_spmd, body=%wide.region_5.8_spmd.sunk | while | flops 345021440 | bytes 13869153 | solution.py:64
  75.1 0.9 fusion.125
  76.0 0.7 fusion.126
  76.7 1.1 fusion.127
  77.8 0.9 fusion.125
  78.7 0.7 fusion.126
  79.4 1.1 fusion.127
  80.6 0.9 fusion.125
  81.5 0.7 fusion.126
  82.2 1.1 fusion.127
  83.3 0.9 fusion.125
  84.2 0.7 fusion.126
  84.9 1.1 fusion.127
  86.1 3.9 %convolution_convert_fusion.1 = bf16[2048,1280]{1,0:T(8,128)(2,1)} fusion(bf16[2048,80]{0,1:T(8,128)(2,1)S(1)} %bitcast.88, bf16[80,1280]{1,0:T(8,128)(2,1)S(1)} %copy-done.3), kind=kOutput, calls=%fused_computation.13 | convolution fusion | flops 422051840 | bytes 5775360 | tf_op jit(solution)/shard_map/dot_general | solution.py:70
  90.0 0.0 reduce-scatter.3.cloned.1.call-update
  90.0 0.0 all-gather.5.cloned.1.call-start
  90.0 78.7 %reduce-scatter.3.cloned.1.call-done = bf16[128,1280]{1,0:T(8,128)(2,1)} async-done(((bf16[2048,1280]{1,0:T(8,128)(2,1)}), bf16[128,1280]{1,0:T(8,128)(2,1)}) %reduce-scatter.3.cloned.1.call-update) | async-done | bytes 327696 | tf_op jit(solution)/shard_map/reduce_scatter | solution.py:69
  168.8 0.0 copy-done.1
  168.8 1.2 convert_reduce_fusion
  170.0 0.2 fusion.56
  170.2 1.0 fusion.58
  171.2 0.0 all-gather.5.cloned.1.call-update
  171.2 0.2 reduce-scatter.5.cloned.1.call-start
  171.4 55.5 %all-gather.5.cloned.1.call-done = bf16[2048,1280]{1,0:T(8,128)(2,1)} async-done(((bf16[128,1280]{1,0:T(8,128)(2,1)}), bf16[2048,1280]{1,0:T(8,128)(2,1)}) %all-gather.5.cloned.1.call-update) | async-done | bytes 5242896 | tf_op jit(solution)/shard_map/all_gather | solution.py:79
  226.9 0.0 copy-done
  226.9 13.4 %convolution_convert_fusion = bf16[2048,1280]{1,0:T(8,128)(2,1)} fusion(bf16[320,1280]{1,0:T(8,128)(2,1)S(1)} %copy-done, bf16[2048,1280]{1,0:T(8,128)(2,1)} %all-gather.5.cloned.1.call-done, bf16[1280,320]{0,1:T(8,128)(2,1)S(1)} %copy-done.6), kind=kOutput, calls=%fused_computation.12 | convolution fusion | flops 3400663040 | bytes 12124160 | tf_op jit(solution)/shard_map/dot_general | solution.py:87
  240.3 0.0 reduce-scatter.5.cloned.1.call-update
  240.3 0.6 copy-done.7
  241.0 0.2 convert_reduce_fusion.2
  241.2 0.1 select_reduce_fusion
  241.3 0.7 sub.48
  242.0 5.3 %all-to-all-start = ((s32[16,1,2]{2,1,0:T(1,128)}), s32[16,1,2]{2,1,0:T(1,128)S(1)}, u32[]{:S(2)}, u32[]{:S(2)}) async-start(s32[16,1,2]{2,1,0:T(1,128)} %bitcast.9), calls=%async_computation | async-start | bytes 16384 | tf_op jit(solution)/shard_map/all_to_all | solution.py:115
  247.3 71.8 %reduce-scatter.5.cloned.1.call-done = bf16[128,1280]{1,0:T(8,128)(2,1)} async-done(((bf16[2048,1280]{1,0:T(8,128)(2,1)}), bf16[128,1280]{1,0:T(8,128)(2,1)}) %reduce-scatter.5.cloned.1.call-update) | async-done | bytes 327696 | tf_op jit(solution)/shard_map/reduce_scatter | solution.py:86
  319.1 1.0 fusion.63
  320.1 0.2 reshape.112
  320.3 0.2 convolution_convert_fusion.2
  320.6 0.8 reshape.113
  321.4 0.0 all-to-all-done
  321.4 4.9 %all-to-all-start.1 = ((bf16[16,2,5120]{2,1,0:T(2,128)(2,1)}), bf16[16,2,5120]{2,1,0:T(2,128)(2,1)S(1)}, u32[]{:S(2)}, u32[]{:S(2)}) async-start(bf16[16,2,5120]{2,1,0:T(2,128)(2,1)} %reshape.113), calls=%async_computation.3 | async-start | bytes 655360 | tf_op jit(solution)/shard_map/all_to_all | solution.py:108
  326.4 0.7 reduce.8
  327.1 0.1 eq.69
  327.1 0.1 fusion.64
  327.2 7.9 %all-to-all-done.1 = bf16[16,2,5120]{2,1,0:T(2,128)(2,1)S(1)} async-done(((bf16[16,2,5120]{2,1,0:T(2,128)(2,1)}), bf16[16,2,5120]{2,1,0:T(2,128)(2,1)S(1)}, u32[]{:S(2)}, u32[]{:S(2)}) %all-to-all-start.1) | async-done | bytes 327712 | tf_op jit(solution)/shard_map/all_to_all | solution.py:108
  335.2 0.1 reshape.114
  335.3 0.0 copy-done.2
  335.3 8.0 %fusion.18 = bf16[128,1280]{1,0:T(8,128)(2,1)} fusion(bf16[128,1280]{1,0:T(8,128)(2,1)S(1)} %copy-done.2, bf16[32,5120]{1,0:T(8,128)(2,1)S(1)} %reshape.114, bf16[5120,1280]{1,0:T(8,128)(2,1)} %param.21, pred[128]{0:T(512)(128)(4,1)S(1)} %fusion.64, s32[32]{0:T(128)S(1)} %eq.69), kind=kOutput, calls=%fused_computation.35 | convolution fusion | flops 430288896 | bytes 14090496 | tf_op jit(solution)/shard_map/dot_general | solution.py:123
  (24 shorter events, 0.2 us)
Async XLA Ops:
  6.5 220.4 %copy-start = (bf16[320,1280]{1,0:T(8,128)(2,1)S(1)}, bf16[320,1280]{1,0:T(8,128)(2,1)}, u32[]{:S(2)}) copy-start(bf16[320,1280]{1,0:T(8,128)(2,1)} %param.20) | copy-start | bytes 2457604
  6.5 63.2 %all-gather.3.cloned.1.call-start = ((), (), s32[]{:S(2)}) async-start(), calls=%async_computation.4 | async-start | bytes 5570560 | tf_op jit(solution)/shard_map/all_gather | solution.py:41
  10.9 157.9 %reduce-scatter.3.cloned.1.call-start = ((), (), s32[]{:S(2)}) async-start(), calls=%async_computation.5 | async-start | bytes 5570560 | tf_op jit(solution)/shard_map/reduce_scatter | solution.py:69
  74.1 0.9 copy-start.4
  75.0 11.0 %copy-start.3 = (bf16[80,1280]{1,0:T(8,128)(2,1)S(1)}, bf16[80,1280]{1,0:T(8,128)(2,1)}, u32[]{:S(2)}) copy-start(bf16[80,1280]{1,0:T(8,128)(2,1)} %param.17) | copy-start | bytes 614404
  90.0 78.8 %copy-start.1 = (bf16[1,128,1280]{2,1,0:T(8,128)(2,1)S(1)}, bf16[1,128,1280]{2,1,0:T(8,128)(2,1)}, u32[]{:S(2)}) copy-start(bf16[1,128,1280]{2,1,0:T(8,128)(2,1)} %param.13) | copy-start | bytes 983044
  90.0 80.2 %copy-start.5 = (f32[1280]{0:T(1024)S(1)}, f32[1280]{0:T(1024)}, u32[]{:S(2)}) copy-start(f32[1280]{0:T(1024)} %param.18) | copy-start | bytes 15364
  90.0 137.0 %copy-start.6 = (bf16[1280,320]{0,1:T(8,128)(2,1)S(1)}, bf16[1280,320]{0,1:T(8,128)(2,1)}, u32[]{:S(2)}) copy-start(bf16[1280,320]{0,1:T(8,128)(2,1)} %param.19) | copy-start | bytes 2457604
  90.0 136.9 %all-gather.5.cloned.1.call-start = ((), (), s32[]{:S(2)}) async-start(), calls=%async_computation.6 | async-start | bytes 5570560 | tf_op jit(solution)/shard_map/all_gather | solution.py:79
  171.2 147.9 %reduce-scatter.5.cloned.1.call-start = ((), (), s32[]{:S(2)}) async-start(), calls=%async_computation.7 | async-start | bytes 5570560 | tf_op jit(solution)/shard_map/reduce_scatter | solution.py:86
  240.3 0.7 copy-start.7
  241.0 94.3 %copy-start.2 = (bf16[128,1280]{1,0:T(8,128)(2,1)S(1)}, bf16[128,1280]{1,0:T(8,128)(2,1)}, u32[]{:S(2)}) copy-start(bf16[128,1280]{1,0:T(8,128)(2,1)} %param.22) | copy-start | bytes 983044
  242.0 79.4 %all-to-all-start = ((s32[16,1,2]{2,1,0:T(1,128)}), s32[16,1,2]{2,1,0:T(1,128)S(1)}, u32[]{:S(2)}, u32[]{:S(2)}) async-start(s32[16,1,2]{2,1,0:T(1,128)} %bitcast.9), calls=%async_computation | async-start | bytes 16384 | tf_op jit(solution)/shard_map/all_to_all | solution.py:115
  321.4 13.8 %all-to-all-start.1 = ((bf16[16,2,5120]{2,1,0:T(2,128)(2,1)}), bf16[16,2,5120]{2,1,0:T(2,128)(2,1)S(1)}, u32[]{:S(2)}, u32[]{:S(2)}) async-start(bf16[16,2,5120]{2,1,0:T(2,128)(2,1)} %reshape.113), calls=%async_computation.3 | async-start | bytes 655360 | tf_op jit(solution)/shard_map/all_to_all | solution.py:108
Sparse Core Ops, SparseCore 0:
  11.0 58.7 all-gather.2
  90.1 78.6 reduce-scatter.2
  171.3 55.5 all-gather.4
  240.5 78.5 reduce-scatter.4
where the time goes:
time: 350 us
  waiting for transfers between devices  271 us (77%)
  matrix products  37.6 us (11%)
  between operations  13.3 us (4%)
  other arithmetic  13.2 us (4%)
  starting transfers between devices  10.5 us (3%)
  local copies, waits for them, and re-layouts  4.15 us (1%)
    reduce_scatter x1, waiting for transfers between devices, local(): lax.psum_scatter(jnp.dot(piece, w_out, preferred_element_type=jnp.float32...  78.7 us
    reduce_scatter x1, waiting for transfers between devices, local(): lax.psum_scatter(jnp.dot(piece, w_down, preferred_element_type=jnp.float3...  71.8 us
    all_gather x1, waiting for transfers between devices, local(): lax.all_gather(normed, 'req', axis=0, tiled=True)  56.8 us
    all_gather x1, waiting for transfers between devices, local(): lax.all_gather(normed_two, 'req', axis=0, tiled=True)  55.5 us
    dot_general x1, matrix products, local(): jnp.dot(piece, w_down, preferred_element_type=jnp.float32)  13.4 us
    dot_general x1, matrix products, local(): jnp.dot(placer.astype(jnp.bfloat16), incoming, preferred_element_type=jnp...  7.96 us
    all_to_all x1, waiting for transfers between devices, local(): lax.all_to_all(outgoing.reshape(req_count, slot_cap, -1), 'req', split_ax...  7.94 us
  transfers between devices with their start and end apart: 6, of which 5 were waited for; matrix products, arithmetic and copies ran while one was open for 2% of the time, Pallas kernels for 0%

commit v1 on v0

--- a/solution.py
+++ b/solution.py
@@ -1,3 +1,4 @@
+import functools
 import math
 import jax
 import jax.numpy as jnp
@@ -5,6 +6,17 @@
 from jax.sharding import PartitionSpec as P
 
 HEAD = 80
+
+
+def plan_tokens(packet, dev_axis):
+    items = []
+    for _ in range(lax.psum(1, dev_axis)):
+        items.append(packet)
+    x_new = jnp.concatenate(lax.all_to_all(jnp.stack(items, axis=0), dev_axis, 0, 0), axis=0)
+    return x_new
+
+
+_create_table = functools.partial(plan_tokens, dev_axis="req")
 
 
 def layer_norm(rows, gain):
@@ -37,10 +49,7 @@
     row_count = lax.axis_size("row")
     normed = layer_norm(rows, ln_attn).astype(jnp.bfloat16)
     qkv = jnp.einsum(
-        "rd,tdc->trc",
-        lax.all_gather(normed, "req", axis=0, tiled=True),
-        w_qkv,
-        preferred_element_type=jnp.float32,
+        "rd,tdc->trc", _create_table(normed), w_qkv, preferred_element_type=jnp.float32
     ).astype(jnp.bfloat16)
     keys = qkv[1]
     values = qkv[2]

time: 350 us -> 388 us (1.11)
  waiting for transfers between devices: 271 us -> 300 us
  starting transfers between devices: 10.5 us -> 17.8 us
    all_to_all x0 -> x1, waiting for transfers between devices: none -> 77.7 us  [plan_tokens(): lax.all_to_all(jnp.stack(items, axis=0), dev_axis, 0, 0)]
    all_gather x1 -> x0, waiting for transfers between devices: 56.8 us -> none  [local(): lax.all_gather(normed, 'req', axis=0, tiled=True)]
    reduce_scatter x1, waiting for transfers between devices: 78.7 us -> 86.6 us  [local(): lax.psum_scatter(jnp.dot(piece, w_out, preferred_element_type=jnp.float32...]
    all_to_all x0 -> x1, starting transfers between devices: none -> 7.29 us  [plan_tokens(): lax.all_to_all(jnp.stack(items, axis=0), dev_axis, 0, 0)]
  transfers between devices with their start and end apart: 6 -> 6, of which waited for: 5 -> 5; matrix products, arithmetic and copies ran while one was open for 2% -> 1% of each run, Pallas kernels for 0% -> 0%
where the time goes in v1:
time: 388 us; the launch traced here: 387 us
  waiting for transfers between devices  300 us (77%)
  matrix products  37.4 us (10%)
  starting transfers between devices  17.8 us (5%)
  between operations  13.3 us (3%)
  other arithmetic  11.8 us (3%)
  local copies, waits for them, and re-layouts  7.01 us (2%)
    reduce_scatter x1, waiting for transfers between devices, local(): lax.psum_scatter(jnp.dot(piece, w_out, preferred_element_type=jnp.float32...  86.6 us
    all_to_all x1, waiting for transfers between devices, plan_tokens(): lax.all_to_all(jnp.stack(items, axis=0), dev_axis, 0, 0)  77.7 us
    reduce_scatter x1, waiting for transfers between devices, local(): lax.psum_scatter(jnp.dot(piece, w_down, preferred_element_type=jnp.float3...  71.8 us
    all_gather x1, waiting for transfers between devices, local(): lax.all_gather(normed_two, 'req', axis=0, tiled=True)  55.6 us
    dot_general x1, matrix products, local(): jnp.dot(piece, w_down, preferred_element_type=jnp.float32)  13.4 us
    dot_general x1, matrix products, local(): jnp.dot(placer.astype(jnp.bfloat16), incoming, preferred_element_type=jnp...  7.95 us
    all_to_all x1, waiting for transfers between devices, local(): lax.all_to_all(outgoing.reshape(req_count, slot_cap, -1), 'req', split_ax...  7.94 us
  transfers between devices with their start and end apart: 6, of which 5 were waited for; matrix products, arithmetic and copies ran while one was open for 1% of the time, Pallas kernels for 0%

profile of v1, /device:TPU:0, one launch (start us, length us, event | category | flops | bytes accessed | tf_op | source)
XLA Modules:
  0.0 387.0 jit_solution(3475780468766617884)
XLA Ops:
  6.5 0.0 copy-start
  6.5 1.2 convert_reduce_fusion.1
  7.7 1.2 fusion.58
  8.9 1.2 fusion.64
  10.1 2.9 stack.5
  13.0 7.3 %all-to-all-start.1 = ((bf16[16,128,1280]{2,1,0:T(8,128)(2,1)}), bf16[16,128,1280]{2,1,0:T(8,128)(2,1)}, u32[]{:S(2)}, u32[]{:S(2)}) async-start(bf16[16,128,1280]{2,1,0:T(8,128)(2,1)} %stack.5), calls=%async_computation.1 | async-start | bytes 10485760 | tf_op jit(solution)/shard_map/all_to_all | solution.py:15
  20.3 0.0 reduce-scatter.3.cloned.1.call-start
  20.4 0.6 broadcast.237
  20.9 0.0 copy-done.4
  20.9 0.7 reduce.7
  21.7 77.7 %all-to-all-done.1 = bf16[16,128,1280]{2,1,0:T(8,128)(2,1)} async-done(((bf16[16,128,1280]{2,1,0:T(8,128)(2,1)}), bf16[16,128,1280]{2,1,0:T(8,128)(2,1)}, u32[]{:S(2)}, u32[]{:S(2)}) %all-to-all-start.1) | async-done | bytes 5242912 | tf_op jit(solution)/shard_map/all_to_all | solution.py:15
  99.3 4.0 %fusion.106 = f32[2048,240]{0,1:S(1)} fusion(bf16[2048,1280]{1,0:T(8,128)(2,1)} %bitcast.12, bf16[1280,240]{0,1:T(8,128)(2,1)S(1)} %bitcast.91), kind=kOutput, calls=%fused_computation.162 | convolution fusion | flops 1258291200 | bytes 7823360
  103.4 0.1 convert_bitcast_fusion
  103.5 0.1 slice_bitcast_fusion
  103.6 0.3 copy.29
  103.9 0.3 copy.26
  104.1 0.3 copy.27
  104.4 0.0 copy-start.3
  104.4 10.9 %while.10 = (s32[]{:T(128)}, bf16[4,512,80]{1,2,0:T(8,128)(2,1)S(1)}, s32[4,512]{1,0:T(4,128)S(1)}, s32[1,2048]{1,0:T(1,128)S(1)}, bf16[4,512,80]{2,1,0:T(8,128)...) while((s32[]{:T(128)}, bf16[4,512,80]{1,2,0:T(8,128)(2,1)S(1)}, ...), condition=%wide.region_8.9_spmd, body=%wide.region_5.8_spmd.sunk | while | flops 345021440 | bytes 13869153 | solution.py:73
  104.5 0.9 fusion.126
  105.4 0.7 fusion.127
  106.1 1.1 fusion.128
  107.2 0.9 fusion.126
  108.1 0.7 fusion.127
  108.8 1.1 fusion.128
  109.9 0.9 fusion.126
  110.8 0.7 fusion.127
  111.6 1.1 fusion.128
  112.7 0.9 fusion.126
  113.6 0.7 fusion.127
  114.3 1.1 fusion.128
  115.4 0.0 copy-done.3
  115.4 3.9 %convolution_convert_fusion.1 = bf16[2048,1280]{1,0:T(8,128)(2,1)} fusion(bf16[2048,80]{0,1:T(8,128)(2,1)S(1)} %bitcast.85, bf16[80,1280]{1,0:T(8,128)(2,1)S(1)} %copy-done.3), kind=kOutput, calls=%fused_computation.13 | convolution fusion | flops 422051840 | bytes 5775360 | tf_op jit(solution)/shard_map/dot_general | solution.py:79
  119.3 0.0 reduce-scatter.3.cloned.1.call-update
  119.3 0.0 all-gather.2.cloned.1.call-start
  119.4 86.6 %reduce-scatter.3.cloned.1.call-done = bf16[128,1280]{1,0:T(8,128)(2,1)} async-done(((bf16[2048,1280]{1,0:T(8,128)(2,1)}), bf16[128,1280]{1,0:T(8,128)(2,1)}) %reduce-scatter.3.cloned.1.call-update) | async-done | bytes 327696 | tf_op jit(solution)/shard_map/reduce_scatter | solution.py:78
  206.0 1.1 convert_reduce_fusion
  207.1 0.2 fusion.54
  207.4 0.0 copy-done.5
  207.4 1.0 fusion.56
  208.3 0.0 all-gather.2.cloned.1.call-update
  208.4 0.2 reduce-scatter.5.cloned.1.call-start
  208.6 55.6 %all-gather.2.cloned.1.call-done = bf16[2048,1280]{1,0:T(8,128)(2,1)} async-done(((bf16[128,1280]{1,0:T(8,128)(2,1)}), bf16[2048,1280]{1,0:T(8,128)(2,1)}) %all-gather.2.cloned.1.call-update) | async-done | bytes 5242896 | tf_op jit(solution)/shard_map/all_gather | solution.py:88
  264.1 0.0 copy-done.6
  264.2 13.4 %convolution_convert_fusion = bf16[2048,1280]{1,0:T(8,128)(2,1)} fusion(bf16[320,1280]{1,0:T(8,128)(2,1)S(1)} %copy-done, bf16[2048,1280]{1,0:T(8,128)(2,1)} %all-gather.2.cloned.1.call-done, bf16[1280,320]{0,1:T(8,128)(2,1)S(1)} %copy-done.6), kind=kOutput, calls=%fused_computation.12 | convolution fusion | flops 3400663040 | bytes 12124160 | tf_op jit(solution)/shard_map/dot_general | solution.py:96
  277.5 0.0 reduce-scatter.5.cloned.1.call-update
  277.6 0.6 copy-done.8
  278.2 0.2 convert_reduce_fusion.2
  278.4 0.1 select_reduce_fusion
  278.5 0.7 sub.53
  279.2 5.3 %all-to-all-start = ((s32[16,1,2]{2,1,0:T(1,128)}), s32[16,1,2]{2,1,0:T(1,128)S(1)}, u32[]{:S(2)}, u32[]{:S(2)}) async-start(s32[16,1,2]{2,1,0:T(1,128)} %bitcast.9), calls=%async_computation | async-start | bytes 16384 | tf_op jit(solution)/shard_map/all_to_all | solution.py:124
  284.5 71.8 %reduce-scatter.5.cloned.1.call-done = bf16[128,1280]{1,0:T(8,128)(2,1)} async-done(((bf16[2048,1280]{1,0:T(8,128)(2,1)}), bf16[128,1280]{1,0:T(8,128)(2,1)}) %reduce-scatter.5.cloned.1.call-update) | async-done | bytes 327696 | tf_op jit(solution)/shard_map/reduce_scatter | solution.py:95
  356.3 1.0 fusion.63
  357.3 0.2 reshape.137
  357.5 0.2 convolution_convert_fusion.2
  357.8 0.9 reshape.138
  358.6 0.0 all-to-all-done
  358.6 4.9 %all-to-all-start.2 = ((bf16[16,2,5120]{2,1,0:T(2,128)(2,1)}), bf16[16,2,5120]{2,1,0:T(2,128)(2,1)S(1)}, u32[]{:S(2)}, u32[]{:S(2)}) async-start(bf16[16,2,5120]{2,1,0:T(2,128)(2,1)} %reshape.138), calls=%async_computation.4 | async-start | bytes 655360 | tf_op jit(solution)/shard_map/all_to_all | solution.py:117
  363.6 0.7 reduce.8
  364.3 0.1 eq.69
  364.3 0.1 fusion.65
  364.4 7.9 %all-to-all-done.2 = bf16[16,2,5120]{2,1,0:T(2,128)(2,1)S(1)} async-done(((bf16[16,2,5120]{2,1,0:T(2,128)(2,1)}), bf16[16,2,5120]{2,1,0:T(2,128)(2,1)S(1)}, u32[]{:S(2)}, u32[]{:S(2)}) %all-to-all-start.2) | async-done | bytes 327712 | tf_op jit(solution)/shard_map/all_to_all | solution.py:117
  372.4 0.1 reshape.139
  372.5 7.9 %fusion.18 = bf16[128,1280]{1,0:T(8,128)(2,1)} fusion(bf16[128,1280]{1,0:T(8,128)(2,1)S(1)} %copy-done.2, bf16[32,5120]{1,0:T(8,128)(2,1)S(1)} %reshape.139, bf16[5120,1280]{1,0:T(8,128)(2,1)} %param.21, pred[128]{0:T(512)(128)(4,1)S(1)} %fusion.65, s32[32]{0:T(128)S(1)} %eq.69), kind=kOutput, calls=%fused_computation.35 | convolution fusion | flops 430288896 | bytes 14090496 | tf_op jit(solution)/shard_map/dot_general | solution.py:132
  (26 shorter events, 0.2 us)
Async XLA Ops:
  6.5 257.6 %copy-start = (bf16[320,1280]{1,0:T(8,128)(2,1)S(1)}, bf16[320,1280]{1,0:T(8,128)(2,1)}, u32[]{:S(2)}) copy-start(bf16[320,1280]{1,0:T(8,128)(2,1)} %param.20) | copy-start | bytes 2457604
  13.0 7.9 %copy-start.4 = (s32[1,2048]{1,0:T(1,128)S(1)}, s32[1,2048]{1,0:T(1,128)}, u32[]{:S(2)}) copy-start(s32[1,2048]{1,0:T(1,128)} %param.14) | copy-start | bytes 24580
  13.0 86.3 %copy-start.7 = (bf16[3,1280,80]{1,2,0:T(8,128)(2,1)S(1)}, bf16[3,1280,80]{1,2,0:T(8,128)(2,1)}, u32[]{:S(2)}) copy-start(bf16[3,1280,80]{1,2,0:T(8,128)(2,1)} %param.16) | copy-start | bytes 1843204
  13.0 86.3 %all-to-all-start.1 = ((bf16[16,128,1280]{2,1,0:T(8,128)(2,1)}), bf16[16,128,1280]{2,1,0:T(8,128)(2,1)}, u32[]{:S(2)}, u32[]{:S(2)}) async-start(bf16[16,128,1280]{2,1,0:T(8,128)(2,1)} %stack.5), calls=%async_computation.1 | async-start | bytes 10485760 | tf_op jit(solution)/shard_map/all_to_all | solution.py:15
  20.3 185.7 %reduce-scatter.3.cloned.1.call-start = ((), (), s32[]{:S(2)}) async-start(), calls=%async_computation.5 | async-start | bytes 5570560 | tf_op jit(solution)/shard_map/reduce_scatter | solution.py:78
  104.4 11.0 %copy-start.3 = (bf16[80,1280]{1,0:T(8,128)(2,1)S(1)}, bf16[80,1280]{1,0:T(8,128)(2,1)}, u32[]{:S(2)}) copy-start(bf16[80,1280]{1,0:T(8,128)(2,1)} %param.17) | copy-start | bytes 614404
  119.3 86.7 %copy-start.1 = (bf16[1,128,1280]{2,1,0:T(8,128)(2,1)S(1)}, bf16[1,128,1280]{2,1,0:T(8,128)(2,1)}, u32[]{:S(2)}) copy-start(bf16[1,128,1280]{2,1,0:T(8,128)(2,1)} %param.13) | copy-start | bytes 983044
  119.3 88.1 %copy-start.5 = (f32[1280]{0:T(1024)S(1)}, f32[1280]{0:T(1024)}, u32[]{:S(2)}) copy-start(f32[1280]{0:T(1024)} %param.18) | copy-start | bytes 15364
  119.3 144.8 %copy-start.6 = (bf16[1280,320]{0,1:T(8,128)(2,1)S(1)}, bf16[1280,320]{0,1:T(8,128)(2,1)}, u32[]{:S(2)}) copy-start(bf16[1280,320]{0,1:T(8,128)(2,1)} %param.19) | copy-start | bytes 2457604
  119.3 144.8 %all-gather.2.cloned.1.call-start = ((), (), s32[]{:S(2)}) async-start(), calls=%async_computation.6 | async-start | bytes 5570560 | tf_op jit(solution)/shard_map/all_gather | solution.py:88
  208.4 147.9 %reduce-scatter.5.cloned.1.call-start = ((), (), s32[]{:S(2)}) async-start(), calls=%async_computation.7 | async-start | bytes 5570560 | tf_op jit(solution)/shard_map/reduce_scatter | solution.py:95
  277.5 0.7 copy-start.8
  278.2 94.3 %copy-start.2 = (bf16[128,1280]{1,0:T(8,128)(2,1)S(1)}, bf16[128,1280]{1,0:T(8,128)(2,1)}, u32[]{:S(2)}) copy-start(bf16[128,1280]{1,0:T(8,128)(2,1)} %param.22) | copy-start | bytes 983044
  279.2 79.4 %all-to-all-start = ((s32[16,1,2]{2,1,0:T(1,128)}), s32[16,1,2]{2,1,0:T(1,128)S(1)}, u32[]{:S(2)}, u32[]{:S(2)}) async-start(s32[16,1,2]{2,1,0:T(1,128)} %bitcast.9), calls=%async_computation | async-start | bytes 16384 | tf_op jit(solution)/shard_map/all_to_all | solution.py:124
  358.6 13.8 %all-to-all-start.2 = ((bf16[16,2,5120]{2,1,0:T(2,128)(2,1)}), bf16[16,2,5120]{2,1,0:T(2,128)(2,1)S(1)}, u32[]{:S(2)}, u32[]{:S(2)}) async-start(bf16[16,2,5120]{2,1,0:T(2,128)(2,1)} %reshape.138), calls=%async_computation.4 | async-start | bytes 655360 | tf_op jit(solution)/shard_map/all_to_all | solution.py:117
Sparse Core Ops, SparseCore 0:
  119.4 86.4 reduce-scatter.2
  208.5 55.6 all-gather.1
  277.7 78.5 reduce-scatter.4
